TPU v7x, 32 devices: a whole 2x2x4 slice. The times are simulated.
32 devices in a mesh: grp: 2 (over y), seq: 4 (over z), head: 2 (over x), sub: 2 (over core).
Axes of the slice: x: 2, y: 2, z: 4, core: 2. Of those that a mesh axis runs over, the one named last changes fastest.
Arguments:
- queries: float32 [1536, 2048], P(('grp', 'seq'), ('head', 'sub')), parts along dimension 0, may hold values from -6 to 6
- keys: float32 [1536, 2048], P(('grp', 'seq'), ('head', 'sub')), parts along dimension 0, may hold values from -6 to 6
- values: float32 [1536, 2048], P(('grp', 'seq'), ('head', 'sub')), parts along dimension 0, may hold values from -40 to 40
- opt_queries: float32 [16, 64, 2048], P(('grp', 'seq'), None, ('head', 'sub')), parts along dimension 0, may hold values from -6 to 6
- opt_keys: float32 [16, 64, 2048], P(('grp', 'seq'), None, ('head', 'sub')), parts along dimension 0, may hold values from -6 to 6
- opt_values: float32 [16, 64, 2048], P(('grp', 'seq'), None, ('head', 'sub')), parts along dimension 0, may hold values from -40 to 40
- opt_offsets: int32 [16], P(('grp', 'seq')), parts along dimension 0, may hold values from 0 to 192
- opt_lengths: int32 [16], P(('grp', 'seq')), parts along dimension 0, may hold values from 1 to 64, 320 in all
- norm_gain: float32 [2048], P(('head', 'sub')), may hold values from 0.5 to 2
- out_weight: bfloat16 [2048, 4096], P(('head', 'sub')), may hold values from -0.125 to 0.125
Outputs:
- ctx_out: bfloat16 [1536, 4096], P(('grp', 'seq'), ('head', 'sub')), parts along dimension 0
- opt_out: bfloat16 [16, 64, 4096], P(('grp', 'seq'), None, ('head', 'sub')), parts along dimension 0
There are 2 independent parts, one for each index of `grp`. A program takes and returns all parts, laid end to end along the dimension named above; an argument that names none is the same for every part. Nothing has to cross between parts.
Inputs may be any that keep to these rules, and one draw needn't show every extreme that they name: `opt_lengths`: within each scoring group the 8 lengths sum to 320, and the longest option of each group has exactly 64 tokens in every draw.
All inputs are finite; a program needn't handle non-finite values.
Results may differ from a plain program's by a relative error of at most 0.017.
Values may be sent and summed in bfloat16 or wider, within the bound.
A program may use at most 64 MiB of HBM per device.

v0:
```python
import functools

import jax
import jax.numpy as jnp
from jax import lax
from jax.experimental import pallas as pl
from jax.experimental.pallas import tpu as pltpu
from jax.sharding import PartitionSpec as P

DH = 128
PIECES = 2
PIECE = DH // PIECES
norm_epsilon = 1e-05
MESH = pl.DeviceIdType.MESH
bf16 = jnp.bfloat16
f32 = jnp.float32


def dot(a, b, ca, cb):
    return lax.dot_general(a, b, (((ca,), (cb,)), ((), ())), preferred_element_type=f32)


def kernel(
    sizes,
    q_hbm, k_hbm, v_hbm, oq_hbm, ok_hbm, ov_hbm, offs_hbm, lens_hbm, gain_hbm, w_hbm,
    ctx_out, opt_out,
    q_buf, k_buf, v_buf, state, intra, pre_recv, pre_send, normed, sib_normed,
    w_own, w_sib, part_send, part_recv, own_part,
    offs, lens, gain_ref,
    in_sem, w_sem, ws_send, ws_recv, pre_ssem, pre_rsem, n_send, n_recv, x_send, x_recv,
):
    n_seq, n_head, n_sub, rows, opts, slots, chunks = sizes
    features = q_hbm.shape[1]
    heads = features // DH
    total = rows + opts * slots
    columns = w_own.shape[2]
    width = columns // chunks
    seq = lax.axis_index("seq")
    head = lax.axis_index("head")
    sub = lax.axis_index("sub")

    barrier = pltpu.get_barrier_semaphore()
    for e in range(1, n_sub):
        pl.semaphore_signal(
            barrier, inc=1, device_id={"sub": lax.rem(sub + e, n_sub)}, device_id_type=MESH
        )
    for d in range(1, n_head):
        pl.semaphore_signal(
            barrier, inc=1, device_id={"head": lax.rem(head + d, n_head)}, device_id_type=MESH
        )

    @pl.when(seq > 0)
    def _():
        pl.semaphore_signal(barrier, inc=1, device_id={"seq": seq - 1}, device_id_type=MESH)

    @pl.when(seq < n_seq - 1)
    def _():
        pl.semaphore_signal(barrier, inc=1, device_id={"seq": seq + 1}, device_id_type=MESH)

    loads = []
    for i, (src, dst, at, count) in enumerate((
        (k_hbm, k_buf, 0, rows),
        (v_hbm, v_buf, 0, rows),
        (q_hbm, q_buf, 0, rows),
        (ok_hbm, k_buf, rows, opts * slots),
        (oq_hbm, q_buf, rows, opts * slots),
        (ov_hbm, v_buf, rows, opts * slots),
    )):
        copy = pltpu.make_async_copy(src, dst.at[pl.ds(at, count)], in_sem.at[i])
        copy.start()
        loads.append(copy)
    for i, (src, dst) in enumerate(((offs_hbm, offs), (lens_hbm, lens), (gain_hbm, gain_ref))):
        copy = pltpu.make_async_copy(src, dst, in_sem.at[6 + i])
        copy.start()
        loads.append(copy)

    def block_of(d, s):
        place = lax.rem(head + d, n_head) * n_sub + s
        return pl.ds(pl.multiple_of(place * columns, columns), columns)

    own_loads = []
    for d in range(n_head):
        copy = pltpu.make_async_copy(w_hbm.at[:, block_of(d, sub)], w_own.at[d], w_sem.at[d])
        own_loads.append(copy)

    def head_cols(h):
        return slice(h * DH, (h + 1) * DH)

    loads[0].wait()
    loads[1].wait()
    for h in range(heads):
        kh = k_buf[:rows, head_cols(h)].astype(bf16)
        vh = v_buf[:rows, head_cols(h)].astype(bf16)
        state[h] = dot(kh, vh, 0, 0)

    @pl.when(seq == 0)
    def _():
        for h in range(heads):
            pre_recv[h] = jnp.zeros((DH, DH), bf16)
            pre_send[h] = state[h].astype(bf16)

    greeted = (n_sub - 1) + (n_head - 1)
    around = jnp.where(seq > 0, 1, 0) + jnp.where(seq < n_seq - 1, 1, 0)
    pl.semaphore_wait(barrier, greeted + around)

    def pre_copy(h, p):
        return pltpu.make_async_remote_copy(
            src_ref=pre_send.at[h, pl.ds(p * PIECE, PIECE)],
            dst_ref=pre_recv.at[h, pl.ds(p * PIECE, PIECE)],
            send_sem=pre_ssem.at[h, p],
            recv_sem=pre_rsem.at[h, p],
            device_id={"seq": seq + 1},
            device_id_type=MESH,
        )

    @pl.when(jnp.logical_and(seq == 0, seq < n_seq - 1))
    def _():
        for h in range(heads):
            for p in range(PIECES):
                pre_copy(h, p).start()

    sib_copies = []
    for d in list(range(1, n_head)) + [0]:
        for e in range(1, n_sub):
            other = lax.rem(sub + e, n_sub)
            copy = pltpu.make_async_remote_copy(
                src_ref=w_hbm.at[:, block_of(d, other)],
                dst_ref=w_sib.at[e - 1, d],
                send_sem=ws_send.at[e - 1, d],
                recv_sem=ws_recv.at[e - 1, d],
                device_id={"sub": other},
                device_id_type=MESH,
            )
            copy.start()
            sib_copies.append(copy)
    for d in list(range(1, n_head)) + [0]:
        own_loads[d].start()

    for i in range(2, 9):
        loads[i].wait()

    ctx_mask = (
        lax.broadcasted_iota(jnp.int32, (rows, rows), 0)
        >= lax.broadcasted_iota(jnp.int32, (rows, rows), 1)
    )
    opt_masks = []
    for o in range(opts):
        col = lax.broadcasted_iota(jnp.int32, (slots, total), 1)
        row = lax.broadcasted_iota(jnp.int32, (slots, total), 0)
        first = rows + o * slots
        here = jnp.logical_and(col >= first, col <= row + first)
        opt_masks.append(jnp.logical_or(col < jnp.minimum(offs[o], rows), here))
    def relay(h):
        for p in range(PIECES):
            pre_copy(h, p).wait_recv()

            @pl.when(seq < n_seq - 1)
            def _():
                at = slice(p * PIECE, (p + 1) * PIECE)
                pre_send[h, at] = (state[h, at] + pre_recv[h, at].astype(f32)).astype(bf16)
                pre_copy(h, p).start()

    for h in range(heads):
        qh = q_buf[:, head_cols(h)].astype(bf16)
        kh = k_buf[:, head_cols(h)].astype(bf16)
        vh = v_buf[:, head_cols(h)].astype(bf16)
        scores = jnp.where(ctx_mask, dot(qh[:rows], kh[:rows], 1, 1), 0.0)
        intra[h, :rows] = dot(scores.astype(bf16), vh[:rows], 1, 0)
        opt_scores = dot(qh[rows:], kh, 1, 1)
        opt_scores = jnp.concatenate([
            jnp.where(opt_masks[o], opt_scores[o * slots:(o + 1) * slots], 0.0)
            for o in range(opts)
        ])
        intra[h, rows:] = dot(opt_scores.astype(bf16), vh, 1, 0)

        @pl.when(seq == 1)
        def _():
            relay(h)

    slot = lax.broadcasted_iota(jnp.int32, (slots, DH), 0)
    valid = [jnp.where(slot < lens[o], 1.0, 0.0) for o in range(opts)]

    n_copies = []
    for h in range(heads):
        @pl.when(seq > 1)
        def _():
            relay(h)

        qh = q_buf[:, head_cols(h)].astype(bf16)
        att = intra[h] + dot(qh, pre_recv[h], 1, 0)
        square = jnp.mean(att * att, axis=-1, keepdims=True)
        out = att * lax.rsqrt(square + norm_epsilon) * gain_ref[:, head_cols(h)]
        normed[:rows, head_cols(h)] = out[:rows].astype(bf16)
        for o in range(opts):
            at = slice(rows + o * slots, rows + (o + 1) * slots)
            normed[at, head_cols(h)] = (out[at] * valid[o]).astype(bf16)
        for e in range(1, n_sub):
            copy = pltpu.make_async_remote_copy(
                src_ref=normed.at[:, pl.ds(h * DH, DH)],
                dst_ref=sib_normed.at[e - 1, :, pl.ds(h * DH, DH)],
                send_sem=n_send.at[e - 1, h],
                recv_sem=n_recv.at[e - 1, h],
                device_id={"sub": lax.rem(sub + e, n_sub)},
                device_id_type=MESH,
            )
            copy.start()
            n_copies.append(copy)

    for d in range(n_head):
        own_loads[d].wait()
    for copy in sib_copies:
        copy.wait_recv()
    for copy in n_copies:
        copy.wait_recv()

    def project(d, c):
        at = pl.ds(c * width, width)
        result = dot(normed[...], w_own[d, :, at], 1, 0)
        for e in range(n_sub - 1):
            result = result + dot(sib_normed[e], w_sib[e, d, :, at], 1, 0)
        return result

    x_copies = {}
    for c in range(chunks):
        for d in range(1, n_head):
            part_send[d - 1, c] = project(d, c).astype(bf16)
            copy = pltpu.make_async_remote_copy(
                src_ref=part_send.at[d - 1, c],
                dst_ref=part_recv.at[d - 1, c],
                send_sem=x_send.at[d - 1, c],
                recv_sem=x_recv.at[d - 1, c],
                device_id={"head": lax.rem(head + d, n_head)},
                device_id_type=MESH,
            )
            copy.start()
            x_copies[d, c] = copy
    for c in range(chunks):
        own_part[c] = project(0, c)
    for c in range(chunks):
        result = own_part[c]
        for d in range(1, n_head):
            x_copies[d, c].wait_recv()
            result = result + part_recv[d - 1, c].astype(f32)
        at = slice(c * width, (c + 1) * width)
        ctx_out[:, at] = result[:rows].astype(bf16)
        opt_out[:, at] = result[rows:].astype(bf16)

    for copy in list(x_copies.values()) + n_copies + sib_copies:
        copy.wait_send()

    @pl.when(seq < n_seq - 1)
    def _():
        for h in range(heads):
            for p in range(PIECES):
                pre_copy(h, p).wait_send()


def write_out(ctx, opt, ctx_hbm, opt_hbm, out_sem):
    copies = [
        pltpu.make_async_copy(ctx, ctx_hbm, out_sem.at[0]),
        pltpu.make_async_copy(opt, opt_hbm, out_sem.at[1]),
    ]
    for copy in copies:
        copy.start()
    for copy in copies:
        copy.wait()


def on_device(
    queries, keys, values, opt_queries, opt_keys, opt_values,
    opt_offsets, opt_lengths, norm_gain, out_weight,
):
    n_seq, n_head, n_sub = (lax.axis_size(a) for a in ("seq", "head", "sub"))
    rows, features = queries.shape
    opts, slots, _ = opt_queries.shape
    heads = features // DH
    total = rows + opts * slots
    columns = out_weight.shape[1] // (n_head * n_sub)
    width = 256 if columns % 256 == 0 else columns
    chunks = columns // width
    flat = lambda a: a.reshape(opts * slots, features)
    anyspace = pl.BlockSpec(memory_space=pl.ANY)
    vmem = pl.BlockSpec(memory_space=pltpu.VMEM)
    sem = pltpu.SemaphoreType.DMA
    ctx, opt = pl.pallas_call(
        functools.partial(kernel, (n_seq, n_head, n_sub, rows, opts, slots, chunks)),
        out_shape=(
            pltpu.VMEM((rows, columns), bf16),
            pltpu.VMEM((opts * slots, columns), bf16),
        ),
        in_specs=[anyspace] * 10,
        out_specs=(vmem, vmem),
        scratch_shapes=[
            pltpu.VMEM((total, features), f32),
            pltpu.VMEM((total, features), f32),
            pltpu.VMEM((total, features), f32),
            pltpu.VMEM((heads, DH, DH), f32),
            pltpu.VMEM((heads, total, DH), f32),
            pltpu.VMEM((heads, DH, DH), bf16),
            pltpu.VMEM((heads, DH, DH), bf16),
            pltpu.VMEM((total, features), bf16),
            pltpu.VMEM((n_sub - 1, total, features), bf16),
            pltpu.VMEM((n_head, features, columns), bf16),
            pltpu.VMEM((n_sub - 1, n_head, features, columns), bf16),
            pltpu.VMEM((n_head - 1, chunks, total, width), bf16),
            pltpu.VMEM((n_head - 1, chunks, total, width), bf16),
            pltpu.VMEM((chunks, total, width), f32),
            pltpu.SMEM((opts,), jnp.int32),
            pltpu.SMEM((opts,), jnp.int32),
            pltpu.VMEM((1, features), f32),
            sem((9,)),
            sem((n_head,)),
            sem((n_sub - 1, n_head)),
            sem((n_sub - 1, n_head)),
            sem((heads, PIECES)),
            sem((heads, PIECES)),
            sem((n_sub - 1, heads)),
            sem((n_sub - 1, heads)),
            sem((n_head - 1, chunks)),
            sem((n_head - 1, chunks)),
        ],
        compiler_params=pltpu.CompilerParams(collective_id=0, has_side_effects=True),
        name="scoring",
    )(
        queries, keys, values, flat(opt_queries), flat(opt_keys), flat(opt_values),
        opt_offsets, opt_lengths, norm_gain.reshape(1, features), out_weight,
    )
    ctx, opt = pl.pallas_call(
        write_out,
        out_shape=(
            jax.ShapeDtypeStruct((rows, columns), bf16),
            jax.ShapeDtypeStruct((opts * slots, columns), bf16),
        ),
        in_specs=[anyspace, anyspace],
        out_specs=(anyspace, anyspace),
        scratch_shapes=[sem((2,))],
        compiler_params=pltpu.CompilerParams(vmem_limit_bytes=1 << 20),
        name="write_out",
    )(ctx, opt)
    return ctx, opt.reshape(opts, slots, columns)


def solution(mesh):
    placed = (
        P(("grp", "seq"), ("head", "sub")),
        P(("grp", "seq"), ("head", "sub")),
        P(("grp", "seq"), ("head", "sub")),
        P(("grp", "seq"), None, ("head", "sub")),
        P(("grp", "seq"), None, ("head", "sub")),
        P(("grp", "seq"), None, ("head", "sub")),
        P(("grp", "seq")),
        P(("grp", "seq")),
        P(("head", "sub")),
        P(("head", "sub"), None),
    )
    return jax.shard_map(
        on_device,
        mesh=mesh,
        in_specs=placed,
        out_specs=(P(("grp", "seq"), ("head", "sub")), P(("grp", "seq"), None, ("head", "sub"))),
        check_vma=False,
    )
```

profile of v0, /device:TPU:25, one launch (start us, length us, event | category | flops | bytes accessed | tf_op | source)
XLA Modules:
  0.0 30.1 jit_solution(15438627832860287626)
XLA Ops:
  0.6 28.6 %scoring.1 = (bf16[192,1024]{1,0:T(8,128)(2,1)S(1)}, bf16[128,1024]{1,0:T(8,128)(2,1)S(1)}) custom-call(f32[192,512]{1,0:T(8,128)} %q_hbm.1, f32[192,512]{1,0:T(8,128)} %k_hbm.1, f32[192,512]{1,0:T(8,128)} %v_hbm.1, f32[128,512]{1,0:T(8,128)} %bitcast.5, f32[128,512]{1,0:T(8,128)} %bitcast.6, f32[128,512]{1,0:T(8,128)} %bitcast.7, s32[2]{0:T(128)} %offs_hbm.1, ...), custom_call_target="tpu_custom_call" | custom-call | tf_op jit(solution)/shard_map/scoring/pallas_call | solution.py:285
  29.3 0.9 %write_out.1 = (bf16[192,1024]{1,0:T(8,128)(2,1)}, bf16[128,1024]{1,0:T(8,128)(2,1)}) custom-call(bf16[192,1024]{1,0:T(8,128)(2,1)S(1)} %get-tuple-element.6.ctx, bf16[128,1024]{1,0:T(8,128)(2,1)S(1)} %get-tuple-element.7.opt), custom_call_target="tpu_custom_call" | custom-call | tf_op jit(solution)/shard_map/write_out/pallas_call | solution.py:328
where the time goes:
time: 30.3 us; the launch traced here: 30.1 us
  Pallas kernels  29.5 us (97%)
  between operations  0.64 us (2%)
    pallas_call x1, Pallas kernels, on_device(): pl.pallas_call(functools.partial(kernel, (n_seq, n_head, n_sub, rows, opt...  28.6 us
    pallas_call x1, Pallas kernels, on_device(): pl.pallas_call(write_out, out_shape=(jax.ShapeDtypeStruct((rows, columns)...  0.85 us

commit v1 on v0

--- a/solution.py
+++ b/solution.py
@@ -10,6 +10,8 @@
 DH = 128
 PIECES = 2
 PIECE = DH // PIECES
+PARTS = 4
+END = 384
 norm_epsilon = 1e-05
 MESH = pl.DeviceIdType.MESH
 bf16 = jnp.bfloat16
@@ -255,6 +257,399 @@
                 pre_copy(h, p).wait_send()
 
 
+def shared_kernel(
+    sizes,
+    q_hbm, k_hbm, v_hbm, oq_hbm, ok_hbm, ov_hbm, offs_hbm, lens_hbm, gain_hbm, w_hbm,
+    ctx_out, opt_out,
+    q_buf, k_buf, v_buf, state, intra, pre_recv, pre_send, normed, sib_normed, far_normed,
+    w_own, w_sib, w_own_end, w_sib_end, w_far, part_send, part_recv, acc,
+    offs, lens, gain_ref,
+    in_sem, w_sem, ws_send, ws_recv, pre_ssem, pre_rsem, n_send, n_recv,
+    f_send, f_recv, r_send, r_recv, x_send, x_recv,
+    wx_send, wf_recv, wy_send, wz_send, wd_send,
+):
+    n_seq, rows, opts, slots, near = sizes
+    features = q_hbm.shape[1]
+    heads = features // DH
+    total = rows + opts * slots
+    columns = w_own.shape[1]
+    end = columns - near
+    parts = w_far.shape[2]
+    band = DH // parts
+    grp = lax.axis_index("grp")
+    seq = lax.axis_index("seq")
+    head = lax.axis_index("head")
+    sub = lax.axis_index("sub")
+    parity = lax.rem(seq, 2)
+    mate = seq + 1 - 2 * parity
+    sibling = {"sub": 1 - sub}
+    across = {"head": 1 - head}
+    beside = {"grp": 1 - grp}
+    along = {"seq": mate}
+    own_q = 2 * grp + parity
+    y_q = 2 * (1 - grp) + parity
+    z_q = 2 * grp + 1 - parity
+    d_q = 2 * (1 - grp) + 1 - parity
+
+    barrier = pltpu.get_barrier_semaphore()
+    pl.semaphore_signal(barrier, inc=1, device_id=sibling, device_id_type=MESH)
+    pl.semaphore_signal(barrier, inc=1, device_id=beside, device_id_type=MESH)
+    for t in range(2):
+        pl.semaphore_signal(
+            barrier, inc=1, device_id={"head": 1 - head, "sub": t}, device_id_type=MESH
+        )
+
+    @pl.when(seq > 0)
+    def _():
+        pl.semaphore_signal(barrier, inc=1, device_id={"seq": seq - 1}, device_id_type=MESH)
+
+    @pl.when(seq < n_seq - 1)
+    def _():
+        pl.semaphore_signal(barrier, inc=1, device_id={"seq": seq + 1}, device_id_type=MESH)
+
+    loads = []
+    for i, (src, dst, at, count) in enumerate((
+        (k_hbm, k_buf, 0, rows),
+        (v_hbm, v_buf, 0, rows),
+        (q_hbm, q_buf, 0, rows),
+        (ok_hbm, k_buf, rows, opts * slots),
+        (oq_hbm, q_buf, rows, opts * slots),
+        (ov_hbm, v_buf, rows, opts * slots),
+    )):
+        copy = pltpu.make_async_copy(src, dst.at[pl.ds(at, count)], in_sem.at[i])
+        copy.start()
+        loads.append(copy)
+    for i, (src, dst) in enumerate(((offs_hbm, offs), (lens_hbm, lens), (gain_hbm, gain_ref))):
+        copy = pltpu.make_async_copy(src, dst, in_sem.at[6 + i])
+        copy.start()
+        loads.append(copy)
+
+    def block_of(h, s, start, count):
+        return pl.ds(pl.multiple_of((h * 2 + s) * columns + start, 128), count)
+
+    def remote(src, dst, send, recv, where):
+        return pltpu.make_async_remote_copy(
+            src_ref=src, dst_ref=dst, send_sem=send, recv_sem=recv,
+            device_id=where, device_id_type=MESH,
+        )
+
+    def head_cols(h):
+        return slice(h * DH, (h + 1) * DH)
+
+    around = jnp.where(seq > 0, 1, 0) + jnp.where(seq < n_seq - 1, 1, 0)
+    pl.semaphore_wait(barrier, 4 + around)
+
+    wx_copies = []
+    for i in range(parts):
+        for t in range(2):
+            at = pl.ds(pl.multiple_of(own_q * DH + i * band, band), band)
+            copy = remote(
+                w_hbm.at[at, block_of(1 - head, t, 0, near)], w_far.at[own_q, sub, i],
+                wx_send.at[t, i], wf_recv.at[own_q, sub, i], {"head": 1 - head, "sub": t},
+            )
+            copy.start()
+            wx_copies.append(copy)
+
+    def arrived(q, s, i):
+        piece = w_far.at[q, s, i]
+        remote(piece, piece, wx_send.at[0, 0], wf_recv.at[q, s, i], across).wait_recv()
+
+    def pass_on(q, s, i, send, where):
+        piece = w_far.at[q, s, i]
+        return remote(piece, piece, send, wf_recv.at[q, s, i], where)
+
+    def y_copy(s, i):
+        return pass_on(own_q, s, i, wy_send.at[s, i], beside)
+
+    def z_copy(s, i):
+        return pass_on(own_q, s, i, wz_send.at[s, i], along)
+
+    def d_copy(s, i):
+        if i % 2 == 0:
+            return pass_on(y_q, s, i, wd_send.at[s, i], along)
+        return pass_on(z_q, s, i, wd_send.at[s, i], beside)
+
+    def own_event(i):
+        for s in range(2):
+            arrived(own_q, s, i)
+            y_copy(s, i).start()
+            z_copy(s, i).start()
+
+    def next_event(i):
+        for s in range(2):
+            arrived(y_q, s, i)
+            if i % 2 == 0:
+                d_copy(s, i).start()
+        for s in range(2):
+            arrived(z_q, s, i)
+            if i % 2 == 1:
+                d_copy(s, i).start()
+
+    loads[0].wait()
+    loads[1].wait()
+    for h in range(heads):
+        kh = k_buf[:rows, head_cols(h)].astype(bf16)
+        vh = v_buf[:rows, head_cols(h)].astype(bf16)
+        state[h] = dot(kh, vh, 0, 0)
+
+    def pre_copy(h, p):
+        return remote(
+            pre_send.at[h, pl.ds(p * PIECE, PIECE)], pre_recv.at[h, pl.ds(p * PIECE, PIECE)],
+            pre_ssem.at[h, p], pre_rsem.at[h, p], {"seq": seq + 1},
+        )
+
+    @pl.when(seq == 0)
+    def _():
+        for h in range(heads):
+            pre_recv[h] = jnp.zeros((DH, DH), bf16)
+            pre_send[h] = state[h].astype(bf16)
+        for h in range(heads):
+            for p in range(PIECES):
+                pre_copy(h, p).start()
+
+    sib_copies = [
+        remote(
+            w_hbm.at[:, block_of(head, 1 - sub, 0, columns)], w_sib,
+            ws_send.at[0], ws_recv.at[0], sibling,
+        ),
+        remote(
+            w_hbm.at[:, block_of(1 - head, 1 - sub, near, end)], w_sib_end,
+            ws_send.at[1], ws_recv.at[1], sibling,
+        ),
+    ]
+    own_loads = [
+        pltpu.make_async_copy(w_hbm.at[:, block_of(head, sub, 0, columns)], w_own, w_sem.at[0]),
+        pltpu.make_async_copy(
+            w_hbm.at[:, block_of(1 - head, sub, near, end)], w_own_end, w_sem.at[1]
+        ),
+    ]
+    for copy in sib_copies + own_loads:
+        copy.start()
+
+    for i in range(2, 9):
+        loads[i].wait()
+
+    ctx_mask = (
+        lax.broadcasted_iota(jnp.int32, (rows, rows), 0)
+        >= lax.broadcasted_iota(jnp.int32, (rows, rows), 1)
+    )
+    opt_masks = []
+    for o in range(opts):
+        col = lax.broadcasted_iota(jnp.int32, (slots, total), 1)
+        row = lax.broadcasted_iota(jnp.int32, (slots, total), 0)
+        first = rows + o * slots
+        here = jnp.logical_and(col >= first, col <= row + first)
+        opt_masks.append(jnp.logical_or(col < jnp.minimum(offs[o], rows), here))
+
+    def relay(h):
+        for p in range(PIECES):
+            pre_copy(h, p).wait_recv()
+
+            @pl.when(seq < n_seq - 1)
+            def _():
+                at = slice(p * PIECE, (p + 1) * PIECE)
+                pre_send[h, at] = (state[h, at] + pre_recv[h, at].astype(f32)).astype(bf16)
+                pre_copy(h, p).start()
+
+    for h in range(heads):
+        qh = q_buf[:, head_cols(h)].astype(bf16)
+        kh = k_buf[:, head_cols(h)].astype(bf16)
+        vh = v_buf[:, head_cols(h)].astype(bf16)
+        scores = jnp.where(ctx_mask, dot(qh[:rows], kh[:rows], 1, 1), 0.0)
+        intra[h, :rows] = dot(scores.astype(bf16), vh[:rows], 1, 0)
+        opt_scores = dot(qh[rows:], kh, 1, 1)
+        opt_scores = jnp.concatenate([
+            jnp.where(opt_masks[o], opt_scores[o * slots:(o + 1) * slots], 0.0)
+            for o in range(opts)
+        ])
+        intra[h, rows:] = dot(opt_scores.astype(bf16), vh, 1, 0)
+
+        @pl.when(seq == 1)
+        def _():
+            relay(h)
+
+    slot = lax.broadcasted_iota(jnp.int32, (slots, DH), 0)
+    valid = [jnp.where(slot < lens[o], 1.0, 0.0) for o in range(opts)]
+
+    @pl.when(seq > 1)
+    def _():
+        own_event(0)
+
+    n_copies = []
+    f_copies = []
+    for h in range(heads):
+        @pl.when(seq > 1)
+        def _():
+            relay(h)
+
+        qh = q_buf[:, head_cols(h)].astype(bf16)
+        att = intra[h] + dot(qh, pre_recv[h], 1, 0)
+        square = jnp.mean(att * att, axis=-1, keepdims=True)
+        out = att * lax.rsqrt(square + norm_epsilon) * gain_ref[:, head_cols(h)]
+        normed[:rows, head_cols(h)] = out[:rows].astype(bf16)
+        for o in range(opts):
+            at = slice(rows + o * slots, rows + (o + 1) * slots)
+            normed[at, head_cols(h)] = (out[at] * valid[o]).astype(bf16)
+        place = pl.ds(pl.multiple_of(sub * DH, DH), DH)
+        copy = remote(
+            normed.at[:, pl.ds(h * DH, DH)], far_normed.at[h, :, place],
+            f_send.at[h], f_recv.at[h], across,
+        )
+        copy.start()
+        f_copies.append(copy)
+        copy = remote(
+            normed.at[:, pl.ds(h * DH, DH)], sib_normed.at[:, pl.ds(h * DH, DH)],
+            n_send.at[h], n_recv.at[h], sibling,
+        )
+        copy.start()
+        n_copies.append(copy)
+        if h == 0:
+            @pl.when(seq > 2)
+            def _():
+                own_event(1)
+
+    @pl.when(seq < 2)
+    def _():
+        own_event(0)
+
+    @pl.when(seq < 3)
+    def _():
+        own_event(1)
+
+    own_event(2)
+
+    for copy in own_loads:
+        copy.wait()
+    for copy in sib_copies + n_copies:
+        copy.wait_recv()
+
+    result = dot(normed[...], w_own_end[...], 1, 0) + dot(sib_normed[...], w_sib_end[...], 1, 0)
+    part_send[...] = result.astype(bf16)
+    x_copy = remote(part_send, part_recv, x_send.at[0], x_recv.at[0], across)
+    x_copy.start()
+
+    next_event(0)
+    step = 256 if columns % 256 == 0 else columns
+    for c in range(0, columns, step):
+        at = slice(c, c + step)
+        acc[:, at] = dot(normed[...], w_own[:, at], 1, 0) + dot(sib_normed[...], w_sib[:, at], 1, 0)
+    own_event(3)
+    for i in range(4, parts):
+        own_event(i)
+
+    r_copies = []
+
+    def hand_over(h):
+        f_copies[h].wait_recv()
+        piece = far_normed.at[h, :, place]
+        copy = remote(piece, piece, r_send.at[h], r_recv.at[h], sibling)
+        copy.start()
+        r_copies.append(copy)
+
+    for i in range(1, parts - 1):
+        next_event(i)
+    hand_over(0)
+    next_event(parts - 1)
+    for h in range(1, heads):
+        hand_over(h)
+    for i in range(parts):
+        for s in range(2):
+            arrived(d_q, s, i)
+    other = pl.ds(pl.multiple_of((1 - sub) * DH, DH), DH)
+    for h in range(heads):
+        piece = far_normed.at[h, :, other]
+        remote(piece, piece, r_send.at[h], r_recv.at[h], sibling).wait_recv()
+
+    for c in range(0, near, step):
+        at = slice(c, min(c + step, near))
+        result = acc[:, at]
+        for h in range(heads):
+            weight = w_far[h, :, :, :, at].reshape(2 * DH, at.stop - at.start)
+            result = result + dot(far_normed[h], weight, 1, 0)
+        ctx_out[:, at] = result[:rows].astype(bf16)
+        opt_out[:, at] = result[rows:].astype(bf16)
+    x_copy.wait_recv()
+    result = acc[:, near:] + part_recv[...].astype(f32)
+    ctx_out[:, near:] = result[:rows].astype(bf16)
+    opt_out[:, near:] = result[rows:].astype(bf16)
+
+    for copy in wx_copies + sib_copies + n_copies + f_copies + r_copies + [x_copy]:
+        copy.wait_send()
+    for s in range(2):
+        for i in range(parts):
+            y_copy(s, i).wait_send()
+            z_copy(s, i).wait_send()
+            d_copy(s, i).wait_send()
+
+    @pl.when(seq < n_seq - 1)
+    def _():
+        for h in range(heads):
+            for p in range(PIECES):
+                pre_copy(h, p).wait_send()
+
+
+def shared_call(n_seq, rows, opts, slots, features, columns):
+    heads = features // DH
+    total = rows + opts * slots
+    near = columns - END
+    sem = pltpu.SemaphoreType.DMA
+    anyspace = pl.BlockSpec(memory_space=pl.ANY)
+    vmem = pl.BlockSpec(memory_space=pltpu.VMEM)
+    return pl.pallas_call(
+        functools.partial(shared_kernel, (n_seq, rows, opts, slots, near)),
+        out_shape=(
+            pltpu.VMEM((rows, columns), bf16),
+            pltpu.VMEM((opts * slots, columns), bf16),
+        ),
+        in_specs=[anyspace] * 10,
+        out_specs=(vmem, vmem),
+        scratch_shapes=[
+            pltpu.VMEM((total, features), f32),
+            pltpu.VMEM((total, features), f32),
+            pltpu.VMEM((total, features), f32),
+            pltpu.VMEM((heads, DH, DH), f32),
+            pltpu.VMEM((heads, total, DH), f32),
+            pltpu.VMEM((heads, DH, DH), bf16),
+            pltpu.VMEM((heads, DH, DH), bf16),
+            pltpu.VMEM((total, features), bf16),
+            pltpu.VMEM((total, features), bf16),
+            pltpu.VMEM((heads, total, 2 * DH), bf16),
+            pltpu.VMEM((features, columns), bf16),
+            pltpu.VMEM((features, columns), bf16),
+            pltpu.VMEM((features, END), bf16),
+            pltpu.VMEM((features, END), bf16),
+            pltpu.VMEM((heads, 2, PARTS, DH // PARTS, near), bf16),
+            pltpu.VMEM((total, END), bf16),
+            pltpu.VMEM((total, END), bf16),
+            pltpu.VMEM((total, columns), f32),
+            pltpu.SMEM((opts,), jnp.int32),
+            pltpu.SMEM((opts,), jnp.int32),
+            pltpu.VMEM((1, features), f32),
+            sem((9,)),
+            sem((2,)),
+            sem((2,)),
+            sem((2,)),
+            sem((heads, PIECES)),
+            sem((heads, PIECES)),
+            sem((heads,)),
+            sem((heads,)),
+            sem((heads,)),
+            sem((heads,)),
+            sem((heads,)),
+            sem((heads,)),
+            sem((1,)),
+            sem((1,)),
+            sem((2, PARTS)),
+            sem((heads, 2, PARTS)),
+            sem((2, PARTS)),
+            sem((2, PARTS)),
+            sem((2, PARTS)),
+        ],
+        compiler_params=pltpu.CompilerParams(collective_id=0, has_side_effects=True),
+        name="scoring",
+    )
+
+
 def write_out(ctx, opt, ctx_hbm, opt_hbm, out_sem):
     copies = [
         pltpu.make_async_copy(ctx, ctx_hbm, out_sem.at[0]),
@@ -282,46 +677,54 @@
     anyspace = pl.BlockSpec(memory_space=pl.ANY)
     vmem = pl.BlockSpec(memory_space=pltpu.VMEM)
     sem = pltpu.SemaphoreType.DMA
-    ctx, opt = pl.pallas_call(
-        functools.partial(kernel, (n_seq, n_head, n_sub, rows, opts, slots, chunks)),
-        out_shape=(
-            pltpu.VMEM((rows, columns), bf16),
-            pltpu.VMEM((opts * slots, columns), bf16),
-        ),
-        in_specs=[anyspace] * 10,
-        out_specs=(vmem, vmem),
-        scratch_shapes=[
-            pltpu.VMEM((total, features), f32),
-            pltpu.VMEM((total, features), f32),
-            pltpu.VMEM((total, features), f32),
-            pltpu.VMEM((heads, DH, DH), f32),
-            pltpu.VMEM((heads, total, DH), f32),
-            pltpu.VMEM((heads, DH, DH), bf16),
-            pltpu.VMEM((heads, DH, DH), bf16),
-            pltpu.VMEM((total, features), bf16),
-            pltpu.VMEM((n_sub - 1, total, features), bf16),
-            pltpu.VMEM((n_head, features, columns), bf16),
-            pltpu.VMEM((n_sub - 1, n_head, features, columns), bf16),
-            pltpu.VMEM((n_head - 1, chunks, total, width), bf16),
-            pltpu.VMEM((n_head - 1, chunks, total, width), bf16),
-            pltpu.VMEM((chunks, total, width), f32),
-            pltpu.SMEM((opts,), jnp.int32),
-            pltpu.SMEM((opts,), jnp.int32),
-            pltpu.VMEM((1, features), f32),
-            sem((9,)),
-            sem((n_head,)),
-            sem((n_sub - 1, n_head)),
-            sem((n_sub - 1, n_head)),
-            sem((heads, PIECES)),
-            sem((heads, PIECES)),
-            sem((n_sub - 1, heads)),
-            sem((n_sub - 1, heads)),
-            sem((n_head - 1, chunks)),
-            sem((n_head - 1, chunks)),
-        ],
-        compiler_params=pltpu.CompilerParams(collective_id=0, has_side_effects=True),
-        name="scoring",
-    )(
+    shared = (
+        lax.axis_size("grp") == 2 and n_head == 2 and n_sub == 2 and n_seq % 2 == 0
+        and heads == 4 and columns > END
+    )
+    if shared:
+        scoring = shared_call(n_seq, rows, opts, slots, features, columns)
+    else:
+        scoring = pl.pallas_call(
+            functools.partial(kernel, (n_seq, n_head, n_sub, rows, opts, slots, chunks)),
+            out_shape=(
+                pltpu.VMEM((rows, columns), bf16),
+                pltpu.VMEM((opts * slots, columns), bf16),
+            ),
+            in_specs=[anyspace] * 10,
+            out_specs=(vmem, vmem),
+            scratch_shapes=[
+                pltpu.VMEM((total, features), f32),
+                pltpu.VMEM((total, features), f32),
+                pltpu.VMEM((total, features), f32),
+                pltpu.VMEM((heads, DH, DH), f32),
+                pltpu.VMEM((heads, total, DH), f32),
+                pltpu.VMEM((heads, DH, DH), bf16),
+                pltpu.VMEM((heads, DH, DH), bf16),
+                pltpu.VMEM((total, features), bf16),
+                pltpu.VMEM((n_sub - 1, total, features), bf16),
+                pltpu.VMEM((n_head, features, columns), bf16),
+                pltpu.VMEM((n_sub - 1, n_head, features, columns), bf16),
+                pltpu.VMEM((n_head - 1, chunks, total, width), bf16),
+                pltpu.VMEM((n_head - 1, chunks, total, width), bf16),
+                pltpu.VMEM((chunks, total, width), f32),
+                pltpu.SMEM((opts,), jnp.int32),
+                pltpu.SMEM((opts,), jnp.int32),
+                pltpu.VMEM((1, features), f32),
+                sem((9,)),
+                sem((n_head,)),
+                sem((n_sub - 1, n_head)),
+                sem((n_sub - 1, n_head)),
+                sem((heads, PIECES)),
+                sem((heads, PIECES)),
+                sem((n_sub - 1, heads)),
+                sem((n_sub - 1, heads)),
+                sem((n_head - 1, chunks)),
+                sem((n_head - 1, chunks)),
+            ],
+            compiler_params=pltpu.CompilerParams(collective_id=0, has_side_effects=True),
+            name="scoring",
+        )
+    ctx, opt = scoring(
         queries, keys, values, flat(opt_queries), flat(opt_keys), flat(opt_values),
         opt_offsets, opt_lengths, norm_gain.reshape(1, features), out_weight,
     )

time: 30.3 us -> 27.9 us (0.921)
  the two profiles are of different devices: /device:TPU:25 before, /device:TPU:0 now
where the time goes in v1:
time: 27.9 us; the launch traced here: 27.4 us
  Pallas kernels  26.8 us (96%)
  between operations  0.64 us (2%)
    pallas_call x1, Pallas kernels, on_device(): scoring(queries, keys, values, flat(opt_queries), flat(opt_keys), flat(op...  25.9 us
    pallas_call x1, Pallas kernels, on_device(): pl.pallas_call(write_out, out_shape=(jax.ShapeDtypeStruct((rows, columns)...  0.85 us

profile of v1, /device:TPU:0, one launch (start us, length us, event | category | flops | bytes accessed | tf_op | source)
XLA Modules:
  0.0 27.4 jit_solution(13858787422204986251)
XLA Ops:
  0.6 25.9 %scoring.1 = (bf16[192,1024]{1,0:T(8,128)(2,1)S(1)}, bf16[128,1024]{1,0:T(8,128)(2,1)S(1)}) custom-call(f32[192,512]{1,0:T(8,128)} %q_hbm.1, f32[192,512]{1,0:T(8,128)} %k_hbm.1, f32[192,512]{1,0:T(8,128)} %v_hbm.1, f32[128,512]{1,0:T(8,128)} %bitcast.5, f32[128,512]{1,0:T(8,128)} %bitcast.6, f32[128,512]{1,0:T(8,128)} %bitcast.7, s32[2]{0:T(128)} %offs_hbm.1, ...), custom_call_target="tpu_custom_call" | custom-call | tf_op jit(solution)/shard_map/scoring/pallas_call | solution.py:727
  26.6 0.9 %write_out.1 = (bf16[192,1024]{1,0:T(8,128)(2,1)}, bf16[128,1024]{1,0:T(8,128)(2,1)}) custom-call(bf16[192,1024]{1,0:T(8,128)(2,1)S(1)} %get-tuple-element.6.ctx, bf16[128,1024]{1,0:T(8,128)(2,1)S(1)} %get-tuple-element.7.opt), custom_call_target="tpu_custom_call" | custom-call | tf_op jit(solution)/shard_map/write_out/pallas_call | solution.py:731

commit v2 on v1

--- a/solution.py
+++ b/solution.py
@@ -12,6 +12,7 @@
 PIECE = DH // PIECES
 PARTS = 4
 END = 384
+WIDTH = 128
 norm_epsilon = 1e-05
 MESH = pl.DeviceIdType.MESH
 bf16 = jnp.bfloat16
@@ -274,6 +275,7 @@
     total = rows + opts * slots
     columns = w_own.shape[1]
     end = columns - near
+    ends, width = part_send.shape[0], part_send.shape[2]
     parts = w_far.shape[2]
     band = DH // parts
     grp = lax.axis_index("grp")
@@ -369,11 +371,13 @@
             return pass_on(y_q, s, i, wd_send.at[s, i], along)
         return pass_on(z_q, s, i, wd_send.at[s, i], beside)
 
-    def own_event(i):
+    def own_event(i, y=True, z=True):
         for s in range(2):
-            arrived(own_q, s, i)
-            y_copy(s, i).start()
-            z_copy(s, i).start()
+            if y:
+                arrived(own_q, s, i)
+                y_copy(s, i).start()
+            if z:
+                z_copy(s, i).start()
 
     def next_event(i):
         for s in range(2):
@@ -464,21 +468,28 @@
         ])
         intra[h, rows:] = dot(opt_scores.astype(bf16), vh, 1, 0)
 
-        @pl.when(seq == 1)
-        def _():
-            relay(h)
 
     slot = lax.broadcasted_iota(jnp.int32, (slots, DH), 0)
     valid = [jnp.where(slot < lens[o], 1.0, 0.0) for o in range(opts)]
 
-    @pl.when(seq > 1)
+    inner = jnp.logical_and(seq > 1, seq < n_seq - 1)
+
+    @pl.when(inner)
+    def _():
+        own_event(0, z=False)
+
+    @pl.when(seq == n_seq - 1)
     def _():
         own_event(0)
+
+    @pl.when(seq > 2)
+    def _():
+        own_event(1)
 
     n_copies = []
     f_copies = []
     for h in range(heads):
-        @pl.when(seq > 1)
+        @pl.when(seq > 0)
         def _():
             relay(h)
 
@@ -503,41 +514,56 @@
         )
         copy.start()
         n_copies.append(copy)
-        if h == 0:
+        if h == 1:
             @pl.when(seq > 2)
             def _():
-                own_event(1)
+                own_event(2)
+
+            @pl.when(inner)
+            def _():
+                own_event(1, z=False)
+
+    @pl.when(inner)
+    def _():
+        own_event(0, y=False)
 
     @pl.when(seq < 2)
     def _():
         own_event(0)
 
-    @pl.when(seq < 3)
+    @pl.when(inner)
+    def _():
+        own_event(1, y=False)
+
+    @pl.when(seq < 2)
     def _():
         own_event(1)
 
-    own_event(2)
-
-    for copy in own_loads:
-        copy.wait()
-    for copy in sib_copies + n_copies:
-        copy.wait_recv()
-
-    result = dot(normed[...], w_own_end[...], 1, 0) + dot(sib_normed[...], w_sib_end[...], 1, 0)
-    part_send[...] = result.astype(bf16)
-    x_copy = remote(part_send, part_recv, x_send.at[0], x_recv.at[0], across)
-    x_copy.start()
-
-    next_event(0)
+    r_copies = []
+    x_copies = [
+        remote(part_send.at[c], part_recv.at[c], x_send.at[c], x_recv.at[c], across)
+        for c in range(ends)
+    ]
     step = 256 if columns % 256 == 0 else columns
-    for c in range(0, columns, step):
-        at = slice(c, c + step)
-        acc[:, at] = dot(normed[...], w_own[:, at], 1, 0) + dot(sib_normed[...], w_sib[:, at], 1, 0)
-    own_event(3)
-    for i in range(4, parts):
-        own_event(i)
-
-    r_copies = []
+
+    def part():
+        for copy in own_loads:
+            copy.wait()
+        for copy in sib_copies + n_copies:
+            copy.wait_recv()
+        for c in range(ends):
+            at = slice(c * width, (c + 1) * width)
+            result = dot(normed[...], w_own_end[:, at], 1, 0)
+            result = result + dot(sib_normed[...], w_sib_end[:, at], 1, 0)
+            part_send[c] = result.astype(bf16)
+            x_copies[c].start()
+
+    def keep(start):
+        for c in range(start * step, columns, 2 * step):
+            at = slice(c, c + step)
+            acc[:, at] = (
+                dot(normed[...], w_own[:, at], 1, 0) + dot(sib_normed[...], w_sib[:, at], 1, 0)
+            )
 
     def hand_over(h):
         f_copies[h].wait_recv()
@@ -546,12 +572,22 @@
         copy.start()
         r_copies.append(copy)
 
-    for i in range(1, parts - 1):
-        next_event(i)
+    @pl.when(seq < 3)
+    def _():
+        own_event(2)
+
+    own_event(3)
+    part()
+    next_event(0)
+    keep(0)
+    next_event(1)
+    keep(1)
+    next_event(2)
+    next_event(3)
     hand_over(0)
-    next_event(parts - 1)
-    for h in range(1, heads):
-        hand_over(h)
+    hand_over(1)
+    hand_over(2)
+    hand_over(3)
     for i in range(parts):
         for s in range(2):
             arrived(d_q, s, i)
@@ -568,12 +604,14 @@
             result = result + dot(far_normed[h], weight, 1, 0)
         ctx_out[:, at] = result[:rows].astype(bf16)
         opt_out[:, at] = result[rows:].astype(bf16)
-    x_copy.wait_recv()
-    result = acc[:, near:] + part_recv[...].astype(f32)
-    ctx_out[:, near:] = result[:rows].astype(bf16)
-    opt_out[:, near:] = result[rows:].astype(bf16)
-
-    for copy in wx_copies + sib_copies + n_copies + f_copies + r_copies + [x_copy]:
+    for c in range(ends):
+        x_copies[c].wait_recv()
+        at = slice(near + c * width, near + (c + 1) * width)
+        result = acc[:, at] + part_recv[c].astype(f32)
+        ctx_out[:, at] = result[:rows].astype(bf16)
+        opt_out[:, at] = result[rows:].astype(bf16)
+
+    for copy in wx_copies + sib_copies + n_copies + f_copies + r_copies + x_copies:
         copy.wait_send()
     for s in range(2):
         for i in range(parts):
@@ -619,8 +657,8 @@
             pltpu.VMEM((features, END), bf16),
             pltpu.VMEM((features, END), bf16),
             pltpu.VMEM((heads, 2, PARTS, DH // PARTS, near), bf16),
-            pltpu.VMEM((total, END), bf16),
-            pltpu.VMEM((total, END), bf16),
+            pltpu.VMEM((END // WIDTH, total, WIDTH), bf16),
+            pltpu.VMEM((END // WIDTH, total, WIDTH), bf16),
             pltpu.VMEM((total, columns), f32),
             pltpu.SMEM((opts,), jnp.int32),
             pltpu.SMEM((opts,), jnp.int32),
@@ -637,8 +675,8 @@
             sem((heads,)),
             sem((heads,)),
             sem((heads,)),
-            sem((1,)),
-            sem((1,)),
+            sem((END // WIDTH,)),
+            sem((END // WIDTH,)),
             sem((2, PARTS)),
             sem((heads, 2, PARTS)),
             sem((2, PARTS)),

time: 27.9 us -> 27.4 us (0.982); the launches traced: 27.4 us -> 27.3 us
  no operation moved by 1% of the time
where the time goes in v2:
time: 27.4 us; the launch traced here: 27.3 us
  Pallas kernels  26.6 us (97%)
  between operations  0.64 us (2%)
    pallas_call x1, Pallas kernels, on_device(): scoring(queries, keys, values, flat(opt_queries), flat(opt_keys), flat(op...  25.8 us
    pallas_call x1, Pallas kernels, on_device(): pl.pallas_call(write_out, out_shape=(jax.ShapeDtypeStruct((rows, columns)...  0.85 us

profile of v2, /device:TPU:0, one launch (start us, length us, event | category | flops | bytes accessed | tf_op | source)
XLA Modules:
  0.0 27.3 jit_solution(3325088341607188837)
XLA Ops:
  0.6 25.8 %scoring.1 = (bf16[192,1024]{1,0:T(8,128)(2,1)S(1)}, bf16[128,1024]{1,0:T(8,128)(2,1)S(1)}) custom-call(f32[192,512]{1,0:T(8,128)} %q_hbm.1, f32[192,512]{1,0:T(8,128)} %k_hbm.1, f32[192,512]{1,0:T(8,128)} %v_hbm.1, f32[128,512]{1,0:T(8,128)} %bitcast.5, f32[128,512]{1,0:T(8,128)} %bitcast.6, f32[128,512]{1,0:T(8,128)} %bitcast.7, s32[2]{0:T(128)} %offs_hbm.1, ...), custom_call_target="tpu_custom_call" | custom-call | tf_op jit(solution)/shard_map/scoring/pallas_call | solution.py:765
  26.4 0.9 %write_out.1 = (bf16[192,1024]{1,0:T(8,128)(2,1)}, bf16[128,1024]{1,0:T(8,128)(2,1)}) custom-call(bf16[192,1024]{1,0:T(8,128)(2,1)S(1)} %get-tuple-element.6.ctx, bf16[128,1024]{1,0:T(8,128)(2,1)S(1)} %get-tuple-element.7.opt), custom_call_target="tpu_custom_call" | custom-call | tf_op jit(solution)/shard_map/write_out/pallas_call | solution.py:769

commit v3 on v2

--- a/solution.py
+++ b/solution.py
@@ -263,7 +263,7 @@
     q_hbm, k_hbm, v_hbm, oq_hbm, ok_hbm, ov_hbm, offs_hbm, lens_hbm, gain_hbm, w_hbm,
     ctx_out, opt_out,
     q_buf, k_buf, v_buf, state, intra, pre_recv, pre_send, normed, sib_normed, far_normed,
-    w_own, w_sib, w_own_end, w_sib_end, w_far, part_send, part_recv, acc,
+    w_own, w_sib, w_own_far, w_sib_far, w_far, part_send, part_recv, acc,
     offs, lens, gain_ref,
     in_sem, w_sem, ws_send, ws_recv, pre_ssem, pre_rsem, n_send, n_recv,
     f_send, f_recv, r_send, r_recv, x_send, x_recv,
@@ -274,8 +274,8 @@
     heads = features // DH
     total = rows + opts * slots
     columns = w_own.shape[1]
-    end = columns - near
-    ends, width = part_send.shape[0], part_send.shape[2]
+    width = part_send.shape[2]
+    chunks, near_chunks = columns // width, near // width
     parts = w_far.shape[2]
     band = DH // parts
     grp = lax.axis_index("grp")
@@ -293,6 +293,11 @@
     z_q = 2 * grp + 1 - parity
     d_q = 2 * (1 - grp) + 1 - parity
 
+    late = seq > 1
+    last = seq == n_seq - 1
+    inner = jnp.logical_and(late, jnp.logical_not(last))
+    early = jnp.logical_not(late)
+
     barrier = pltpu.get_barrier_semaphore()
     pl.semaphore_signal(barrier, inc=1, device_id=sibling, device_id_type=MESH)
     pl.semaphore_signal(barrier, inc=1, device_id=beside, device_id_type=MESH)
@@ -339,18 +344,50 @@
         return slice(h * DH, (h + 1) * DH)
 
     around = jnp.where(seq > 0, 1, 0) + jnp.where(seq < n_seq - 1, 1, 0)
-    pl.semaphore_wait(barrier, 4 + around)
-
     wx_copies = []
     for i in range(parts):
         for t in range(2):
             at = pl.ds(pl.multiple_of(own_q * DH + i * band, band), band)
-            copy = remote(
+            wx_copies.append(remote(
                 w_hbm.at[at, block_of(1 - head, t, 0, near)], w_far.at[own_q, sub, i],
                 wx_send.at[t, i], wf_recv.at[own_q, sub, i], {"head": 1 - head, "sub": t},
-            )
+            ))
+
+    sib_near = remote(
+        w_hbm.at[:, block_of(1 - head, 1 - sub, 0, near)], w_sib_far.at[:, pl.ds(0, near)],
+        ws_send.at[0], ws_recv.at[0], sibling,
+    )
+    sib_copies = [
+        remote(
+            w_hbm.at[:, block_of(1 - head, 1 - sub, near, columns - near)],
+            w_sib_far.at[:, pl.ds(near, columns - near)],
+            ws_send.at[1], ws_recv.at[1], sibling,
+        ),
+        remote(
+            w_hbm.at[:, block_of(head, 1 - sub, 0, columns)], w_sib,
+            ws_send.at[2], ws_recv.at[2], sibling,
+        ),
+    ]
+    own_loads = [
+        pltpu.make_async_copy(
+            w_hbm.at[:, block_of(1 - head, sub, 0, columns)], w_own_far, w_sem.at[0]
+        ),
+        pltpu.make_async_copy(w_hbm.at[:, block_of(head, sub, 0, columns)], w_own, w_sem.at[1]),
+    ]
+
+    pl.semaphore_wait(barrier, 4 + around)
+
+    @pl.when(late)
+    def _():
+        for copy in wx_copies:
             copy.start()
-            wx_copies.append(copy)
+
+    @pl.when(early)
+    def _():
+        sib_near.start()
+
+    sib_copies[0].start()
+    own_loads[0].start()
 
     def arrived(q, s, i):
         piece = w_far.at[q, s, i]
@@ -411,24 +448,8 @@
             for p in range(PIECES):
                 pre_copy(h, p).start()
 
-    sib_copies = [
-        remote(
-            w_hbm.at[:, block_of(head, 1 - sub, 0, columns)], w_sib,
-            ws_send.at[0], ws_recv.at[0], sibling,
-        ),
-        remote(
-            w_hbm.at[:, block_of(1 - head, 1 - sub, near, end)], w_sib_end,
-            ws_send.at[1], ws_recv.at[1], sibling,
-        ),
-    ]
-    own_loads = [
-        pltpu.make_async_copy(w_hbm.at[:, block_of(head, sub, 0, columns)], w_own, w_sem.at[0]),
-        pltpu.make_async_copy(
-            w_hbm.at[:, block_of(1 - head, sub, near, end)], w_own_end, w_sem.at[1]
-        ),
-    ]
-    for copy in sib_copies + own_loads:
-        copy.start()
+    sib_copies[1].start()
+    own_loads[1].start()
 
     for i in range(2, 9):
         loads[i].wait()
@@ -455,67 +476,101 @@
                 pre_send[h, at] = (state[h, at] + pre_recv[h, at].astype(f32)).astype(bf16)
                 pre_copy(h, p).start()
 
-    for h in range(heads):
-        qh = q_buf[:, head_cols(h)].astype(bf16)
+    def inside_ctx(h):
+        qh = q_buf[:rows, head_cols(h)].astype(bf16)
+        kh = k_buf[:rows, head_cols(h)].astype(bf16)
+        vh = v_buf[:rows, head_cols(h)].astype(bf16)
+        scores = jnp.where(ctx_mask, dot(qh, kh, 1, 1), 0.0)
+        intra[h, :rows] = dot(scores.astype(bf16), vh, 1, 0)
+
+    def inside_opt(h):
+        qh = q_buf[rows:, head_cols(h)].astype(bf16)
         kh = k_buf[:, head_cols(h)].astype(bf16)
         vh = v_buf[:, head_cols(h)].astype(bf16)
-        scores = jnp.where(ctx_mask, dot(qh[:rows], kh[:rows], 1, 1), 0.0)
-        intra[h, :rows] = dot(scores.astype(bf16), vh[:rows], 1, 0)
-        opt_scores = dot(qh[rows:], kh, 1, 1)
+        opt_scores = dot(qh, kh, 1, 1)
         opt_scores = jnp.concatenate([
             jnp.where(opt_masks[o], opt_scores[o * slots:(o + 1) * slots], 0.0)
             for o in range(opts)
         ])
         intra[h, rows:] = dot(opt_scores.astype(bf16), vh, 1, 0)
 
-
     slot = lax.broadcasted_iota(jnp.int32, (slots, DH), 0)
     valid = [jnp.where(slot < lens[o], 1.0, 0.0) for o in range(opts)]
 
-    inner = jnp.logical_and(seq > 1, seq < n_seq - 1)
+    spans = ((0, rows), (rows, opts * slots))
+
+    def norm(h, kind):
+        at = slice(spans[kind][0], spans[kind][0] + spans[kind][1])
+        att = intra[h, at] + dot(q_buf[at, head_cols(h)].astype(bf16), pre_recv[h], 1, 0)
+        square = jnp.mean(att * att, axis=-1, keepdims=True)
+        out = att * lax.rsqrt(square + norm_epsilon) * gain_ref[:, head_cols(h)]
+        if kind == 1:
+            out = jnp.concatenate([
+                out[o * slots:(o + 1) * slots] * valid[o] for o in range(opts)
+            ])
+        normed[at, head_cols(h)] = out.astype(bf16)
+
+    def n_copy(h, kind):
+        at = (pl.ds(*spans[kind]), pl.ds(h * DH, DH))
+        return remote(
+            normed.at[at], sib_normed.at[at], n_send.at[kind, h], n_recv.at[kind, h], sibling
+        )
+
+    @pl.when(seq == 0)
+    def _():
+        for kind, inside in enumerate((inside_ctx, inside_opt)):
+            for h in range(heads):
+                inside(h)
+            for h in range(heads):
+                norm(h, kind)
+                n_copy(h, kind).start()
+
+    @pl.when(seq > 0)
+    def _():
+        for h in range(heads):
+            inside_ctx(h)
+            inside_opt(h)
 
     @pl.when(inner)
     def _():
         own_event(0, z=False)
 
-    @pl.when(seq == n_seq - 1)
+    @pl.when(last)
     def _():
         own_event(0)
 
-    @pl.when(seq > 2)
+    @pl.when(last)
     def _():
         own_event(1)
 
-    n_copies = []
-    f_copies = []
+    place = pl.ds(pl.multiple_of(sub * DH, DH), DH)
+    f_copies = [
+        remote(
+            normed.at[:, pl.ds(h * DH, DH)], far_normed.at[h, :, place],
+            f_send.at[h], f_recv.at[h], across,
+        )
+        for h in range(heads)
+    ]
     for h in range(heads):
         @pl.when(seq > 0)
         def _():
             relay(h)
 
-        qh = q_buf[:, head_cols(h)].astype(bf16)
-        att = intra[h] + dot(qh, pre_recv[h], 1, 0)
-        square = jnp.mean(att * att, axis=-1, keepdims=True)
-        out = att * lax.rsqrt(square + norm_epsilon) * gain_ref[:, head_cols(h)]
-        normed[:rows, head_cols(h)] = out[:rows].astype(bf16)
-        for o in range(opts):
-            at = slice(rows + o * slots, rows + (o + 1) * slots)
-            normed[at, head_cols(h)] = (out[at] * valid[o]).astype(bf16)
-        place = pl.ds(pl.multiple_of(sub * DH, DH), DH)
-        copy = remote(
-            normed.at[:, pl.ds(h * DH, DH)], far_normed.at[h, :, place],
-            f_send.at[h], f_recv.at[h], across,
-        )
-        copy.start()
-        f_copies.append(copy)
-        copy = remote(
-            normed.at[:, pl.ds(h * DH, DH)], sib_normed.at[:, pl.ds(h * DH, DH)],
-            n_send.at[h], n_recv.at[h], sibling,
-        )
-        copy.start()
-        n_copies.append(copy)
+        @pl.when(seq == 1)
+        def _():
+            norm(h, 0)
+            n_copy(h, 0).start()
+
+        @pl.when(late)
+        def _():
+            norm(h, 0)
+            norm(h, 1)
+            f_copies[h].start()
+            for kind in range(2):
+                n_copy(h, kind).start()
+
         if h == 1:
-            @pl.when(seq > 2)
+            @pl.when(last)
             def _():
                 own_event(2)
 
@@ -523,101 +578,138 @@
             def _():
                 own_event(1, z=False)
 
-    @pl.when(inner)
-    def _():
-        own_event(0, y=False)
-
-    @pl.when(seq < 2)
-    def _():
-        own_event(0)
-
-    @pl.when(inner)
-    def _():
-        own_event(1, y=False)
-
-    @pl.when(seq < 2)
-    def _():
-        own_event(1)
-
-    r_copies = []
-    x_copies = [
-        remote(part_send.at[c], part_recv.at[c], x_send.at[c], x_recv.at[c], across)
-        for c in range(ends)
-    ]
-    step = 256 if columns % 256 == 0 else columns
-
-    def part():
-        for copy in own_loads:
-            copy.wait()
-        for copy in sib_copies + n_copies:
-            copy.wait_recv()
-        for c in range(ends):
-            at = slice(c * width, (c + 1) * width)
-            result = dot(normed[...], w_own_end[:, at], 1, 0)
-            result = result + dot(sib_normed[...], w_sib_end[:, at], 1, 0)
-            part_send[c] = result.astype(bf16)
-            x_copies[c].start()
-
-    def keep(start):
-        for c in range(start * step, columns, 2 * step):
-            at = slice(c, c + step)
-            acc[:, at] = (
-                dot(normed[...], w_own[:, at], 1, 0) + dot(sib_normed[...], w_sib[:, at], 1, 0)
-            )
-
-    def hand_over(h):
-        f_copies[h].wait_recv()
-        piece = far_normed.at[h, :, place]
-        copy = remote(piece, piece, r_send.at[h], r_recv.at[h], sibling)
-        copy.start()
-        r_copies.append(copy)
-
-    @pl.when(seq < 3)
-    def _():
-        own_event(2)
-
-    own_event(3)
-    part()
-    next_event(0)
-    keep(0)
-    next_event(1)
-    keep(1)
-    next_event(2)
-    next_event(3)
-    hand_over(0)
-    hand_over(1)
-    hand_over(2)
-    hand_over(3)
-    for i in range(parts):
-        for s in range(2):
-            arrived(d_q, s, i)
-    other = pl.ds(pl.multiple_of((1 - sub) * DH, DH), DH)
-    for h in range(heads):
-        piece = far_normed.at[h, :, other]
-        remote(piece, piece, r_send.at[h], r_recv.at[h], sibling).wait_recv()
-
-    for c in range(0, near, step):
-        at = slice(c, min(c + step, near))
-        result = acc[:, at]
-        for h in range(heads):
-            weight = w_far[h, :, :, :, at].reshape(2 * DH, at.stop - at.start)
-            result = result + dot(far_normed[h], weight, 1, 0)
+    @pl.when(seq == 1)
+    def _():
+        for h in range(heads):
+            norm(h, 1)
+            n_copy(h, 1).start()
+
+    def chunk(c, count=1):
+        return slice(c * width, (c + count) * width)
+
+    def x_copy(c, kind):
+        at = pl.ds(*spans[kind])
+        return remote(
+            part_send.at[c, at], part_recv.at[c, at],
+            x_send.at[kind, c], x_recv.at[kind, c], across,
+        )
+
+    def ready(kind):
+        for h in range(heads):
+            n_copy(h, kind).wait_recv()
+
+    def loaded(i):
+        own_loads[i].wait()
+        sib_copies[i].wait_recv()
+
+    def give(c, count, kind):
+        at = chunk(c, count)
+        lines = slice(spans[kind][0], spans[kind][0] + spans[kind][1])
+        result = dot(normed[lines], w_own_far[:, at], 1, 0)
+        result = result + dot(sib_normed[lines], w_sib_far[:, at], 1, 0)
+        for k in range(count):
+            part_send[c + k, lines] = result[:, chunk(k)].astype(bf16)
+            x_copy(c + k, kind).start()
+
+    def keep(c, count):
+        at = chunk(c, count)
+        acc[:, at] = dot(normed[...], w_own[:, at], 1, 0) + dot(sib_normed[...], w_sib[:, at], 1, 0)
+
+    def put(at, result):
         ctx_out[:, at] = result[:rows].astype(bf16)
         opt_out[:, at] = result[rows:].astype(bf16)
-    for c in range(ends):
-        x_copies[c].wait_recv()
-        at = slice(near + c * width, near + (c + 1) * width)
-        result = acc[:, at] + part_recv[c].astype(f32)
-        ctx_out[:, at] = result[:rows].astype(bf16)
-        opt_out[:, at] = result[rows:].astype(bf16)
-
-    for copy in wx_copies + sib_copies + n_copies + f_copies + r_copies + x_copies:
+
+    def take(c, kind):
+        x_copy(c, kind).wait_recv()
+        lines = slice(spans[kind][0], spans[kind][0] + spans[kind][1])
+        result = acc[lines, chunk(c)] + part_recv[c, lines].astype(f32)
+        (ctx_out, opt_out)[kind][:, chunk(c)] = result.astype(bf16)
+
+    step = 256
+    pair = step // width
+
+    @pl.when(early)
+    def _():
+        loaded(0)
+        sib_near.wait_recv()
+        for kind in range(2):
+            ready(kind)
+            for c in range(0, chunks, pair):
+                give(c, pair, kind)
+        loaded(1)
+        for c in range(0, chunks, pair):
+            keep(c, pair)
+        for kind in range(2):
+            for c in range(chunks):
+                take(c, kind)
+        for kind in range(2):
+            for c in range(chunks):
+                x_copy(c, kind).wait_send()
+        sib_near.wait_send()
+
+    r_copies = []
+    for h in range(heads):
+        piece = far_normed.at[h, :, place]
+        r_copies.append(remote(piece, piece, r_send.at[h], r_recv.at[h], sibling))
+
+    @pl.when(late)
+    def _():
+        @pl.when(inner)
+        def _():
+            own_event(0, y=False)
+            own_event(1, y=False)
+            own_event(2)
+
+        own_event(3)
+        loaded(0)
+        loaded(1)
+        for kind in range(2):
+            ready(kind)
+        for c in range(near_chunks, chunks):
+            for kind in range(2):
+                give(c, 1, kind)
+        next_event(0)
+        for c in range(0, chunks, 2 * pair):
+            keep(c, pair)
+        next_event(1)
+        for c in range(pair, chunks, 2 * pair):
+            keep(c, pair)
+        for i in range(2, parts):
+            next_event(i)
+        for h in range(heads):
+            f_copies[h].wait_recv()
+            r_copies[h].start()
+        for i in range(parts):
+            for s in range(2):
+                arrived(d_q, s, i)
+        other = pl.ds(pl.multiple_of((1 - sub) * DH, DH), DH)
+        for h in range(heads):
+            piece = far_normed.at[h, :, other]
+            remote(piece, piece, r_send.at[h], r_recv.at[h], sibling).wait_recv()
+        for c in range(0, near, step):
+            at = slice(c, min(c + step, near))
+            result = acc[:, at]
+            for h in range(heads):
+                weight = w_far[h, :, :, :, at].reshape(2 * DH, at.stop - at.start)
+                result = result + dot(far_normed[h], weight, 1, 0)
+            put(at, result)
+        for c in range(near_chunks, chunks):
+            for kind in range(2):
+                take(c, kind)
+                x_copy(c, kind).wait_send()
+        for copy in wx_copies + f_copies + r_copies:
+            copy.wait_send()
+        for s in range(2):
+            for i in range(parts):
+                y_copy(s, i).wait_send()
+                z_copy(s, i).wait_send()
+                d_copy(s, i).wait_send()
+
+    for copy in sib_copies:
         copy.wait_send()
-    for s in range(2):
-        for i in range(parts):
-            y_copy(s, i).wait_send()
-            z_copy(s, i).wait_send()
-            d_copy(s, i).wait_send()
+    for kind in range(2):
+        for h in range(heads):
+            n_copy(h, kind).wait_send()
 
     @pl.when(seq < n_seq - 1)
     def _():
@@ -654,29 +746,29 @@
             pltpu.VMEM((heads, total, 2 * DH), bf16),
             pltpu.VMEM((features, columns), bf16),
             pltpu.VMEM((features, columns), bf16),
-            pltpu.VMEM((features, END), bf16),
-            pltpu.VMEM((features, END), bf16),
+            pltpu.VMEM((features, columns), bf16),
+            pltpu.VMEM((features, columns), bf16),
             pltpu.VMEM((heads, 2, PARTS, DH // PARTS, near), bf16),
-            pltpu.VMEM((END // WIDTH, total, WIDTH), bf16),
-            pltpu.VMEM((END // WIDTH, total, WIDTH), bf16),
+            pltpu.VMEM((columns // WIDTH, total, WIDTH), bf16),
+            pltpu.VMEM((columns // WIDTH, total, WIDTH), bf16),
             pltpu.VMEM((total, columns), f32),
             pltpu.SMEM((opts,), jnp.int32),
             pltpu.SMEM((opts,), jnp.int32),
             pltpu.VMEM((1, features), f32),
             sem((9,)),
             sem((2,)),
-            sem((2,)),
-            sem((2,)),
+            sem((3,)),
+            sem((3,)),
             sem((heads, PIECES)),
             sem((heads, PIECES)),
+            sem((2, heads)),
+            sem((2, heads)),
             sem((heads,)),
             sem((heads,)),
             sem((heads,)),
             sem((heads,)),
-            sem((heads,)),
-            sem((heads,)),
-            sem((END // WIDTH,)),
-            sem((END // WIDTH,)),
+            sem((2, columns // WIDTH)),
+            sem((2, columns // WIDTH)),
             sem((2, PARTS)),
             sem((heads, 2, PARTS)),
             sem((2, PARTS)),
@@ -717,7 +809,7 @@
     sem = pltpu.SemaphoreType.DMA
     shared = (
         lax.axis_size("grp") == 2 and n_head == 2 and n_sub == 2 and n_seq % 2 == 0
-        and heads == 4 and columns > END
+        and heads == 4 and columns > END and columns % 512 == 0
     )
     if shared:
         scoring = shared_call(n_seq, rows, opts, slots, features, columns)

time: 27.4 us -> 27.1 us (0.989)
  Pallas kernels: 26.6 us -> 26.3 us
    pallas_call x1, Pallas kernels: 25.8 us -> 25.5 us  [on_device(): scoring(queries, keys, values, flat(opt_queries), flat(opt_keys), flat(op...]
where the time goes in v3:
time: 27.1 us; the launch traced here: 27 us
  Pallas kernels  26.3 us (97%)
  between operations  0.64 us (2%)
    pallas_call x1, Pallas kernels, on_device(): scoring(queries, keys, values, flat(opt_queries), flat(opt_keys), flat(op...  25.5 us
    pallas_call x1, Pallas kernels, on_device(): pl.pallas_call(write_out, out_shape=(jax.ShapeDtypeStruct((rows, columns)...  0.85 us

profile of v3, /device:TPU:0, one launch (start us, length us, event | category | flops | bytes accessed | tf_op | source)
XLA Modules:
  0.0 27.0 jit_solution(9979848610579400803)
XLA Ops:
  0.6 25.5 %scoring.1 = (bf16[192,1024]{1,0:T(8,128)(2,1)S(1)}, bf16[128,1024]{1,0:T(8,128)(2,1)S(1)}) custom-call(f32[192,512]{1,0:T(8,128)} %q_hbm.1, f32[192,512]{1,0:T(8,128)} %k_hbm.1, f32[192,512]{1,0:T(8,128)} %v_hbm.1, f32[128,512]{1,0:T(8,128)} %bitcast.5, f32[128,512]{1,0:T(8,128)} %bitcast.6, f32[128,512]{1,0:T(8,128)} %bitcast.7, s32[2]{0:T(128)} %offs_hbm.1, ...), custom_call_target="tpu_custom_call" | custom-call | tf_op jit(solution)/shard_map/scoring/pallas_call | solution.py:857
  26.1 0.9 %write_out.1 = (bf16[192,1024]{1,0:T(8,128)(2,1)}, bf16[128,1024]{1,0:T(8,128)(2,1)}) custom-call(bf16[192,1024]{1,0:T(8,128)(2,1)S(1)} %get-tuple-element.6.ctx, bf16[128,1024]{1,0:T(8,128)(2,1)S(1)} %get-tuple-element.7.opt), custom_call_target="tpu_custom_call" | custom-call | tf_op jit(solution)/shard_map/write_out/pallas_call | solution.py:861
